TPU v7x, 32 devices: a whole 2x2x4 slice. The times are simulated.
32 devices in a mesh: blk: 4 (over x, core), shard: 8 (over z, y).
Axes of the slice: x: 2, y: 2, z: 4, core: 2. Of those that a mesh axis runs over, the one named last changes fastest.
Arguments:
- item_features: bfloat16 [32768, 1024], P('shard'), may hold values from -6 to 6
- tower_weight: bfloat16 [1024, 512], replicated, may hold values from -0.1875 to 0.1875
- gate_in: bfloat16 [64, 128], replicated, may hold values from -0.75 to 0.75
- gate_in_bias: bfloat16 [128], replicated, may hold values from -4 to 4
- gate_out: bfloat16 [128, 64], replicated, may hold values from -0.5 to 0.5
- gate_out_bias: bfloat16 [64], replicated, may hold values from -4 to 4
- user_table: bfloat16 [4096, 512], P(('blk', 'shard')), may hold values from -6 to 6
- user_ids: int32 [128], P(('blk', 'shard')), may hold values from 0 to 127
- positive_item: int32 [128, 16], P(('blk', 'shard')), may hold values from 0 to 2047
- listed_owner: int32 [128, 1], P(('blk', 'shard')), may hold values from 0 to 7; in each aligned block of 4 rows (0 to 3, 4 to 7, ...) at most 2 rows name the same one
- listed_slot: int32 [128], P(('blk', 'shard')), may hold values from 0 to 31
Outputs:
- tower_gradient: float32 [1024, 512], P('shard')
- user_gradient: float32 [4096, 512], P(('blk', 'shard'))
Inputs may be any that keep to these rules, and one draw needn't show every extreme that they name: `listed_owner`: at most 2 of the 4 listings of one trainer name the same owner. `user_ids`: A row of the trainer's own 128 rows of user_table. `positive_item`: A position among the rows of the user's circle.
All inputs are finite; a program needn't handle non-finite values.
Results may differ from a plain program's by a relative error of at most 0.0055.
Values may be sent and summed in bfloat16 or wider, within the bound.
A program may use at most 128 MiB of HBM per device.

v0:
```python
import math

import jax
import jax.numpy as jnp
from jax import lax
from jax.sharding import PartitionSpec as P

K = 8
H = 64
BLK = 128
CAP = 2
OWN = 32
USERS = 4
UTAB = 128
E = 512


def pair_terms(user_rows, item_rows, targets, gate_in, gate_in_bias, gate_out, gate_out_bias):
    count_users = user_rows.shape[0]
    count_items = item_rows.shape[0]
    scaling = 1.0 / math.sqrt(H)
    user_parts = user_rows.reshape(count_users * K, H)
    item_parts = item_rows.reshape(count_items, K, H)
    logits = (
        jnp.einsum("xh,ibh->xbi", user_parts, item_parts, preferred_element_type=jnp.float32)
        * scaling
    )
    logits = logits.reshape(count_users, K * K, count_items)
    gate_input = logits.astype(jnp.bfloat16)
    hidden_pre = jnp.einsum("pg,upi->ugi", gate_in, gate_input, preferred_element_type=jnp.float32)
    hidden_pre = hidden_pre + gate_in_bias.astype(jnp.float32)[None, :, None]
    hidden = jax.nn.silu(hidden_pre).astype(jnp.bfloat16)
    gate_logit = jnp.einsum("gp,ugi->upi", gate_out, hidden, preferred_element_type=jnp.float32)
    gate_logit = gate_logit + gate_out_bias.astype(jnp.float32)[None, :, None]
    exp_terms = jnp.exp(gate_logit)
    mixture = exp_terms / jnp.sum(exp_terms, axis=1, keepdims=True)
    scores = jnp.sum(mixture * logits, axis=1)
    score_grad = jax.nn.sigmoid(scores) - targets
    weighted = score_grad[:, None, :] * mixture
    logit_grad = (weighted * (logits - scores[:, None, :])).astype(jnp.bfloat16)
    gate_sig = jax.nn.sigmoid(hidden_pre)
    hidden_grad = jnp.einsum(
        "gp,upi->ugi", gate_out, logit_grad, preferred_element_type=jnp.float32
    )
    hidden_grad = (hidden_grad * gate_sig * (1.0 + hidden_pre * (1.0 - gate_sig))).astype(
        jnp.bfloat16
    )
    pair_grad = weighted + jnp.einsum(
        "pg,ugi->upi", gate_in, hidden_grad, preferred_element_type=jnp.float32
    )
    pair_grad = pair_grad.astype(jnp.bfloat16).reshape(count_users * K, K, count_items)
    user_delta = jnp.einsum(
        "xbi,ibh->xh", pair_grad, item_parts, preferred_element_type=jnp.float32
    )
    item_delta = jnp.einsum(
        "xbi,xh->ibh", pair_grad, user_parts, preferred_element_type=jnp.float32
    )
    return (
        user_delta.reshape(count_users, K * H) * scaling,
        item_delta.reshape(count_items, K * H) * scaling,
    )


def match_targets(positives, first_column, count):
    columns = first_column + jnp.arange(count, dtype=jnp.int32)
    return jnp.any(positives[:, :, None] == columns[None, None, :], axis=1).astype(jnp.float32)


def split_product(left_bf16, right_f32):
    upper = right_f32.astype(jnp.bfloat16)
    lower = (right_f32 - upper.astype(jnp.float32)).astype(jnp.bfloat16)
    dims = (((0,), (0,)), ((), ()))
    first = lax.dot_general(left_bf16, upper, dims, preferred_element_type=jnp.float32)
    second = lax.dot_general(left_bf16, lower, dims, preferred_element_type=jnp.float32)
    return first + second


def shards(
    item_features,
    tower_weight,
    gate_in,
    gate_in_bias,
    gate_out,
    gate_out_bias,
    user_table,
    user_ids,
    positive_item,
    listed_owner,
    listed_slot,
):
    block_groups = lax.axis_size("blk")
    owner_count = lax.axis_size("shard")
    group_index = lax.axis_index("blk")
    listings = listed_slot.shape[0]
    circle_part = listings * BLK
    owner_ids = listed_owner[:, 0]
    listing_order = jnp.arange(listings, dtype=jnp.int32)
    same_owner = owner_ids[:, None] == owner_ids[None, :]
    earlier = listing_order[None, :] < listing_order[:, None]
    rank_within = jnp.sum(jnp.logical_and(same_owner, earlier), axis=1)
    owner_match = owner_ids[:, None] == jnp.arange(owner_count, dtype=jnp.int32)[None, :]
    rank_match = rank_within[:, None] == jnp.arange(CAP, dtype=jnp.int32)[None, :]
    placement = jnp.logical_and(owner_match[:, :, None], rank_match[:, None, :])
    wanted = jnp.sum(jnp.where(placement, listed_slot[:, None, None] + 1, 0), axis=0) - 1
    asked_slots = lax.all_to_all(wanted, "shard", split_axis=0, concat_axis=0, tiled=True)
    slot_pick = jnp.clip(asked_slots, 0, OWN - 1).reshape(-1)
    slot_of = owner_ids * CAP + rank_within
    own_vectors = jnp.dot(item_features, tower_weight, preferred_element_type=jnp.float32).astype(
        jnp.bfloat16
    )
    own_vectors = own_vectors.reshape(OWN, BLK, E)
    outgoing = jnp.take(own_vectors, slot_pick, axis=0).reshape(owner_count, CAP, BLK, E)
    arrived = lax.all_to_all(outgoing, "shard", split_axis=0, concat_axis=0, tiled=True).reshape(
        owner_count * CAP, BLK, E
    )
    listed = jnp.take(arrived, slot_of, axis=0).reshape(circle_part, E)
    row_match = user_ids[:, None] == jnp.arange(UTAB, dtype=jnp.int32)[None, :]
    user_rows = jnp.dot(
        row_match.astype(jnp.bfloat16), user_table, preferred_element_type=jnp.float32
    ).astype(jnp.bfloat16)
    all_users = lax.all_gather(user_rows, "blk", axis=0, tiled=True)
    all_positive = lax.all_gather(positive_item, "blk", axis=0, tiled=True)
    item_delta = jnp.zeros((circle_part, E), jnp.float32)
    user_terms = []
    for source in range(block_groups):
        source_users = all_users[source * USERS : (source + 1) * USERS]
        source_positive = all_positive[source * USERS : (source + 1) * USERS]
        targets = match_targets(source_positive, group_index * circle_part, circle_part)
        user_term, item_term = pair_terms(
            source_users, listed, targets, gate_in, gate_in_bias, gate_out, gate_out_bias
        )
        user_terms.append(user_term)
        item_delta = item_delta + item_term
    user_delta = lax.psum_scatter(
        jnp.concatenate(user_terms, axis=0), "blk", scatter_dimension=0, tiled=True
    )
    listing_grads = item_delta.astype(jnp.bfloat16)
    returning = jnp.zeros((owner_count * CAP, BLK, E), jnp.bfloat16)
    returning = returning.at[slot_of].set(listing_grads.reshape(listings, BLK, E))
    returned = lax.all_to_all(
        returning.reshape(owner_count, CAP, BLK, E),
        "shard",
        split_axis=0,
        concat_axis=0,
        tiled=True,
    )
    returned = returned.reshape(owner_count * CAP, BLK * E)
    slot_hot = (
        asked_slots.reshape(-1)[None, :] == jnp.arange(OWN, dtype=jnp.int32)[:, None]
    ).astype(jnp.bfloat16)
    summed = jnp.dot(slot_hot, returned, preferred_element_type=jnp.float32).reshape(OWN * BLK, E)
    partial_value = split_product(item_features, summed)
    tower_part = lax.psum_scatter(partial_value, "shard", scatter_dimension=0, tiled=True)
    tower_gradient = lax.psum(tower_part, "blk")
    user_gradient = split_product(row_match.astype(jnp.bfloat16), user_delta)
    return (tower_gradient, user_gradient)


def solution(mesh):
    return jax.shard_map(
        shards,
        mesh=mesh,
        in_specs=(
            P("shard", None),
            P(),
            P(),
            P(),
            P(),
            P(),
            P(("blk", "shard"), None),
            P(("blk", "shard")),
            P(("blk", "shard"), None),
            P(("blk", "shard"), None),
            P(("blk", "shard")),
        ),
        out_specs=(P("shard", None), P(("blk", "shard"), None)),
        check_vma=False,
    )
```

profile of v0, /device:TPU:0, one launch (start us, length us, event | category | flops | bytes accessed | tf_op | source)
XLA Modules:
  0.0 318.4 jit_solution(14100097331826583886)
XLA Ops:
  10.3 7.3 %all-to-all-start = ((s32[8,1,2]{2,1,0:T(1,128)}), s32[8,1,2]{2,1,0:T(1,128)S(1)}, u32[]{:S(2)}, u32[]{:S(2)}) async-start(s32[8,1,2]{2,1,0:T(1,128)} %copy.117), calls=%async_computation | async-start | bytes 8192 | tf_op jit(solution)/shard_map/all_to_all | solution.py:105
  17.6 9.5 %convolution_convert_fusion = bf16[4096,512]{1,0:T(8,128)(2,1)} fusion(bf16[4096,1024]{1,0:T(8,128)(2,1)} %param.11, bf16[1024,512]{1,0:T(8,128)(2,1)S(1)} %copy-done), kind=kOutput, calls=%fused_computation.8 | convolution fusion | flops 4297064448 | bytes 13631488 | tf_op jit(solution)/shard_map/dot_general | solution.py:108
  28.6 2.9 gather_fusion
  31.5 1.6 broadcast_select_fusion
  33.1 6.0 %all-to-all-start.1 = ((bf16[8,2,128,512]{3,2,1,0:T(8,128)(2,1)}), bf16[8,2,128,512]{3,2,1,0:T(8,128)(2,1)S(1)}, u32[]{:S(2)}, u32[]{:S(2)}) async-start(bf16[8,2,128,512]{3,2,1,0:T(8,128)(2,1)} %broadcast_select_fusion), calls=%async_computation.1 | async-start | bytes 4194304 | tf_op jit(solution)/shard_map/all_to_all | solution.py:113
  39.4 5.2 %all-gather = bf16[4,4,512]{2,1,0:T(4,128)(2,1)S(1)} all-gather(bf16[1,4,512]{2,1,0:T(4,128)(2,1)S(1)} %fusion.65), channel_id=1, replica_groups=mesh['blk'=4,'shard'=8] {'blk'}, dimensions={0}, use_global_device_ids=true | all-gather | bytes 20480 | tf_op jit(solution)/shard_map/all_gather | solution.py:121
  44.9 5.4 %all-gather.1 = s32[4,4,16]{2,1,0:T(4,128)S(1)} all-gather(s32[1,4,16]{2,1,0:T(4,128)S(1)} %bitcast.390), channel_id=1, replica_groups=mesh['blk'=4,'shard'=8] {'blk'}, dimensions={0}, use_global_device_ids=true | all-gather | bytes 1280 | tf_op jit(solution)/shard_map/all_gather | solution.py:122
  50.5 36.3 %all-to-all-done.1 = bf16[8,2,128,512]{3,2,1,0:T(8,128)(2,1)S(1)} async-done(((bf16[8,2,128,512]{3,2,1,0:T(8,128)(2,1)}), bf16[8,2,128,512]{3,2,1,0:T(8,128)(2,1)S(1)}, u32[]{:S(2)}, u32[]{:S(2)}) %all-to-all-start.1) | async-done | bytes 2097184 | tf_op jit(solution)/shard_map/all_to_all | solution.py:113
  89.9 1.3 fusion.19
  91.2 1.6 fusion.31
  92.8 1.6 fusion.30
  94.4 1.4 fusion.20
  97.2 1.3 fusion.21
  99.9 1.3 fusion.22
  101.6 2.2 fusion.57
  104.2 1.9 fusion.86
  108.3 2.8 fusion.60
  111.1 2.9 fusion.59
  114.1 2.5 fusion.58
  116.5 1.3 convolution_add_fusion.4
  119.0 1.6 broadcast_in_dim.44
  120.5 2.5 scatter_fusion
  123.0 3.6 %all-to-all-start.2 = ((bf16[8,2,128,512]{3,2,1,0:T(8,128)(2,1)}), bf16[8,2,128,512]{3,2,1,0:T(8,128)(2,1)S(1)}, u32[]{:S(2)}, u32[]{:S(2)}) async-start(bf16[8,2,128,512]{3,2,1,0:T(8,128)(2,1)} %bitcast.47), calls=%async_computation.2 | async-start | bytes 4194304 | tf_op jit(solution)/shard_map/all_to_all | solution.py:140
  127.0 48.1 %all-to-all-done.2 = bf16[8,2,128,512]{3,2,1,0:T(8,128)(2,1)S(1)} async-done(((bf16[8,2,128,512]{3,2,1,0:T(8,128)(2,1)}), bf16[8,2,128,512]{3,2,1,0:T(8,128)(2,1)S(1)}, u32[]{:S(2)}, u32[]{:S(2)}) %all-to-all-start.2) | async-done | bytes 2097184 | tf_op jit(solution)/shard_map/all_to_all | solution.py:140
  176.2 4.5 %fusion.127 = f32[32,65536]{1,0:T(8,128)} fusion(bf16[16,65536]{1,0:T(8,128)(2,1)S(1)} %bitcast.377, s32[16]{0:T(128)S(1)} %eq.130), kind=kOutput, calls=%fused_computation.181 | convolution fusion | flops 67109376 | bytes 10485824 | tf_op jit(solution)/shard_map/dot_general | solution.py:151
  180.7 7.5 %reshape.311 = f32[4096,512]{1,0:T(8,128)} reshape(f32[32,65536]{1,0:T(8,128)} %fusion.127) | data formatting | bytes 16777216 | tf_op jit(solution)/shard_map/reshape | solution.py:151
  188.1 10.8 %fusion.4 = f32[512,1024]{1,0:T(8,128)S(1)} fusion(bf16[4096,1024]{1,0:T(8,128)(2,1)} %param.11, f32[4096,512]{1,0:T(8,128)} %reshape.311), kind=kOutput, calls=%fused_computation.9 | convolution fusion | flops 4303355904 | bytes 18874368 | tf_op jit(solution)/shard_map/dot_general | solution.py:74
  198.9 9.0 %add_bitcast_fusion = f32[1024,512]{0,1:T(8,128)} fusion(f32[512,1024]{1,0:T(8,128)S(1)} %fusion.4, bf16[4096,1024]{1,0:T(8,128)(2,1)} %param.11, f32[4096,512]{1,0:T(8,128)S(1)} %copy-done.2), kind=kOutput, calls=%fused_computation.10 | convolution fusion | flops 4297588736 | bytes 20971520 | tf_op jit(solution)/shard_map/dot_general | solution.py:73
  211.3 10.5 %all-reduce = f32[16,512]{1,0:T(8,128)S(1)} all-reduce(f32[16,512]{1,0:T(8,128)S(1)} %pad_maximum_fusion), channel_id=3, replica_groups=mesh['blk'=4,'shard'=8] {'blk'}, use_global_device_ids=true, to_apply=%region_17.18.clone | all-reduce | flops 8192 | bytes 65536
  222.2 53.9 %reduce-scatter.2.cloned.1.call-done = f32[128,512]{0,1:T(8,128)} async-done(((f32[1024,512]{0,1:T(8,128)}), f32[128,512]{0,1:T(8,128)}) %reduce-scatter.2.cloned.1.call-update) | async-done | bytes 262160 | tf_op jit(solution)/shard_map/reduce_scatter | solution.py:153
  277.1 32.7 %all-reduce.3.cloned.1.call-done = f32[128,512]{0,1:T(8,128)} async-done(((f32[128,512]{0,1:T(8,128)}), f32[128,512]{0,1:T(8,128)}) %all-reduce.3.cloned.1.call-update) | async-done | bytes 262160 | tf_op jit(solution)/shard_map/psum | solution.py:154
  309.8 1.8 copy.143
  (132 shorter events, 20.6 us)
Async XLA Ops:
  7.2 10.4 %copy-start = (bf16[1024,512]{1,0:T(8,128)(2,1)S(1)}, bf16[1024,512]{1,0:T(8,128)(2,1)}, u32[]{:S(2)}) copy-start(bf16[1024,512]{1,0:T(8,128)(2,1)} %param.12) | copy-start | bytes 3145732
  10.3 16.8 %all-to-all-start = ((s32[8,1,2]{2,1,0:T(1,128)}), s32[8,1,2]{2,1,0:T(1,128)S(1)}, u32[]{:S(2)}, u32[]{:S(2)}) async-start(s32[8,1,2]{2,1,0:T(1,128)} %copy.117), calls=%async_computation | async-start | bytes 8192 | tf_op jit(solution)/shard_map/all_to_all | solution.py:105
  31.4 7.7 %copy-start.22 = (bf16[128]{0:T(256)(128)(2,1)S(1)}, bf16[128]{0:T(256)(128)(2,1)}, u32[]{:S(2)}) copy-start(bf16[128]{0:T(256)(128)(2,1)} %param.14) | copy-start | bytes 772
  31.5 7.7 %copy-start.23 = (bf16[64]{0:T(256)(128)(2,1)S(1)}, bf16[64]{0:T(256)(128)(2,1)}, u32[]{:S(2)}) copy-start(bf16[64]{0:T(256)(128)(2,1)} %param.16) | copy-start | bytes 388
  31.5 7.7 %copy-start.18 = (s32[4]{0:T(128)S(1)}, s32[4]{0:T(128)}, u32[]{:S(2)}) copy-start(s32[4]{0:T(128)} %param.18) | copy-start | bytes 52
  31.5 7.7 %copy-start.20 = (bf16[128,512]{1,0:T(8,128)(2,1)S(1)}, bf16[128,512]{1,0:T(8,128)(2,1)}, u32[]{:S(2)}) copy-start(bf16[128,512]{1,0:T(8,128)(2,1)} %param.17) | copy-start | bytes 393220
  31.5 13.4 %copy-start.17 = (s32[4,16]{1,0:T(4,128)S(1)}, s32[4,16]{1,0:T(4,128)}, u32[]{:S(2)}) copy-start(s32[4,16]{1,0:T(4,128)} %param.19) | copy-start | bytes 772
  31.5 18.8 %copy-start.19 = (s32[4,1]{0,1:T(1,128)S(1)}, s32[4,1]{0,1:T(1,128)}, u32[]{:S(2)}) copy-start(s32[4,1]{0,1:T(1,128)} %param.20) | copy-start | bytes 52
  33.1 53.7 %all-to-all-start.1 = ((bf16[8,2,128,512]{3,2,1,0:T(8,128)(2,1)}), bf16[8,2,128,512]{3,2,1,0:T(8,128)(2,1)S(1)}, u32[]{:S(2)}, u32[]{:S(2)}) async-start(bf16[8,2,128,512]{3,2,1,0:T(8,128)(2,1)} %broadcast_select_fusion), calls=%async_computation.1 | async-start | bytes 4194304 | tf_op jit(solution)/shard_map/all_to_all | solution.py:113
  87.4 0.8 copy-start.3
  88.2 1.7 copy-start.11
  88.5 2.7 copy-start.21
  97.2 4.2 %copy-start.7 = (f32[4,64,512]{2,1,0:T(8,128)}, f32[4,64,512]{2,1,0:T(8,128)S(1)}, u32[]{:S(2)}) copy-start(f32[4,64,512]{2,1,0:T(8,128)S(1)} %fusion.29) | copy-start | bytes 1572868
  99.9 1.6 copy-start.9
  101.6 4.4 %copy-start.5 = (f32[4,64,512]{2,1,0:T(8,128)S(1)}, f32[4,64,512]{2,1,0:T(8,128)}, u32[]{:S(2)}) copy-start(f32[4,64,512]{2,1,0:T(8,128)} %fusion.30) | copy-start | bytes 1572868
  103.8 4.3 %copy-start.6 = (f32[4,64,512]{2,1,0:T(8,128)S(1)}, f32[4,64,512]{2,1,0:T(8,128)}, u32[]{:S(2)}) copy-start(f32[4,64,512]{2,1,0:T(8,128)} %fusion.31) | copy-start | bytes 1572868
  111.1 2.9 copy-start.8
  111.1 2.9 copy-start.10
  114.0 3.8 %copy-start.14 = (bf16[4,64,512]{2,1,0:T(8,128)(2,1)S(1)}, bf16[4,64,512]{2,1,0:T(8,128)(2,1)}, u32[]{:S(2)}) copy-start(bf16[4,64,512]{2,1,0:T(8,128)(2,1)} %fusion.59) | copy-start | bytes 786436
  114.0 4.1 %copy-start.12 = (bf16[4,64,512]{2,1,0:T(8,128)(2,1)S(1)}, bf16[4,64,512]{2,1,0:T(8,128)(2,1)}, u32[]{:S(2)}) copy-start(bf16[4,64,512]{2,1,0:T(8,128)(2,1)} %fusion.60) | copy-start | bytes 786436
  123.0 52.1 %all-to-all-start.2 = ((bf16[8,2,128,512]{3,2,1,0:T(8,128)(2,1)}), bf16[8,2,128,512]{3,2,1,0:T(8,128)(2,1)S(1)}, u32[]{:S(2)}, u32[]{:S(2)}) async-start(bf16[8,2,128,512]{3,2,1,0:T(8,128)(2,1)} %bitcast.47), calls=%async_computation.2 | async-start | bytes 4194304 | tf_op jit(solution)/shard_map/all_to_all | solution.py:140
  126.6 149.4 %reduce-scatter.2.cloned.1.call-start = ((), (), s32[]{:S(2)}) async-start(), calls=%async_computation.4 | async-start | bytes 2359296 | tf_op jit(solution)/shard_map/reduce_scatter | solution.py:153
  188.1 10.8 %copy-start.2 = (f32[4096,512]{1,0:T(8,128)S(1)}, f32[4096,512]{1,0:T(8,128)}, u32[]{:S(2)}) copy-start(f32[4096,512]{1,0:T(8,128)} %reshape.311) | copy-start | bytes 25165828
  198.9 9.1 %copy-start.24 = (u32[32]{0:T(128)S(1)}, u32[32]{0:T(128)}, u32[]{:S(2)}) copy-start(u32[32]{0:T(128)} %constant.72) | copy-start | bytes 388
  198.9 10.4 %copy-start.4 = (bf16[4,128,512]{2,1,0:T(8,128)(2,1)S(1)}, bf16[4,128,512]{2,1,0:T(8,128)(2,1)}, u32[]{:S(2)}) copy-start(bf16[4,128,512]{2,1,0:T(8,128)(2,1)} %copy-done.3) | copy-start | bytes 1572868
  207.9 1.9 copy-start.13
  207.9 2.3 copy-start.15
  207.9 2.7 copy-start.16
  207.9 101.9 %all-reduce.3.cloned.1.call-start = ((), (), s32[]{:S(2)}) async-start(), calls=%async_computation.5 | async-start | bytes 524288 | tf_op jit(solution)/shard_map/psum | solution.py:154
  209.2 102.3 %copy-start.1 = (bf16[1024,512]{1,0:T(8,128)(2,1)S(1)}, bf16[1024,512]{1,0:T(8,128)(2,1)}, u32[]{:S(2)}) copy-start(bf16[1024,512]{1,0:T(8,128)(2,1)} %param.12) | copy-start | bytes 3145732
Sparse Core Ops, SparseCore 0:
  208.0 67.9 reduce-scatter.1
  278.4 31.3 all-reduce.2
where the time goes:
time: 319 us; the launch traced here: 318 us
  waiting for transfers between devices  171 us (54%)
  matrix products  59.9 us (19%)
  local copies, waits for them, and re-layouts  24.2 us (8%)
  blocking collectives  21.1 us (7%)
  starting transfers between devices  17.2 us (5%)
  between operations  15.3 us (5%)
  other arithmetic  9.7 us (3%)
    reduce_scatter x1, waiting for transfers between devices, shards(): lax.psum_scatter(partial_value, 'shard', scatter_dimension=0, tiled=True)  53.9 us
    all_to_all x1, waiting for transfers between devices, shards(): lax.all_to_all(returning.reshape(owner_count, CAP, BLK, E), 'shard', spli...  48.1 us
    all_to_all x1, waiting for transfers between devices, shards(): lax.all_to_all(outgoing, 'shard', split_axis=0, concat_axis=0, tiled=True)  36.3 us
    psum x1, waiting for transfers between devices, shards(): tower_gradient = lax.psum(tower_part, 'blk')  32.7 us
    dot_general x2, matrix products, split_product(): lax.dot_general(left_bf16, lower, dims, preferred_element_type=jnp.float32)  11.8 us
    unnamed x1, blocking collectives  10.5 us
    dot_general x4, matrix products, pair_terms(): jnp.einsum('pg,ugi->upi', gate_in, hidden_grad, preferred_element_type=jn...  10.4 us
    dot_general x1, matrix products, shards(): jnp.dot(item_features, tower_weight, preferred_element_type=jnp.float32)  9.49 us
  transfers between devices with their start and end apart: 5, of which 4 were waited for; matrix products, arithmetic and copies ran while one was open for 4% of the time, Pallas kernels for 0%

commit v1 on v0

v1 whole, which is shorter than its diff:
```python
import functools
import math

import jax
import jax.numpy as jnp
from jax import lax
from jax.experimental import pallas as pl
from jax.experimental.pallas import tpu as pltpu
from jax.sharding import PartitionSpec as P

K = 8
H = 64
BLK = 128
CAP = 2
LANES = 128
CHUNK = 4

NN = (((1,), (0,)), ((), ()))
NT = (((1,), (1,)), ((), ()))


def dot(left, right, dims=NN):
    return lax.dot_general(left, right, dims, preferred_element_type=jnp.float32)


def sigmoid(v):
    return 0.5 + 0.5 * jnp.tanh(0.5 * v)


def pair_kernel(
    groups,
    owners,
    users,
    count_ref,
    block_ref,
    column_ref,
    base_ref,
    feat_ref,
    tower_ref,
    users_ref,
    users_t_ref,
    pos_ref,
    gin_ref,
    gin_t_ref,
    gin_b_ref,
    gout_ref,
    gout_t_ref,
    gout_b_ref,
    out_ref,
    acc,
    uacc,
    logit_s,
    pair_s,
):
    step = pl.program_id(0)
    column_users = groups * users
    rows = column_users * K

    @pl.when(step == 0)
    def _():
        acc[...] = jnp.zeros_like(acc)
        uacc[...] = jnp.zeros_like(uacc)

    @pl.when(step < count_ref[0])
    def _():
        column = column_ref[step]
        base = base_ref[step]
        feat = feat_ref[...]
        vec_t = dot(tower_ref[...], feat, NT).astype(jnp.bfloat16)
        vec_cat = jnp.concatenate([vec_t[b * H : (b + 1) * H] for b in range(K)], axis=1)
        logit_s[...] = dot(users_ref[column], vec_cat)
        pos = pos_ref[column]
        place = base + lax.broadcasted_iota(jnp.int32, (column_users, BLK), 1)
        hit = pos[:, 0:1] == place
        for k in range(1, pos.shape[1]):
            hit = jnp.logical_or(hit, pos[:, k : k + 1] == place)
        target = jnp.where(hit, 1.0, 0.0)
        for first in range(0, column_users, CHUNK):
            picked = range(first, first + CHUNK)
            logits = jnp.concatenate(
                [
                    jnp.concatenate(
                        [
                            logit_s[u * K : (u + 1) * K, b * BLK : (b + 1) * BLK]
                            for b in range(K)
                        ],
                        axis=0,
                    )
                    for u in picked
                ],
                axis=1,
            )
            wanted = jnp.concatenate([target[u : u + 1] for u in picked], axis=1)
            pre = dot(gin_t_ref[...], logits.astype(jnp.bfloat16)) + gin_b_ref[...]
            sig = sigmoid(pre)
            silu = pre * sig
            slope = sig + silu * (1.0 - sig)
            gate = dot(gout_t_ref[...], silu.astype(jnp.bfloat16)) + gout_b_ref[...]
            terms = jnp.exp(gate)
            mixture = terms * (1.0 / jnp.sum(terms, axis=0, keepdims=True))
            scores = jnp.sum(mixture * logits, axis=0, keepdims=True)
            score_grad = sigmoid(scores) - wanted
            weighted = score_grad * mixture
            logit_grad = (weighted * (logits - scores)).astype(jnp.bfloat16)
            hidden_grad = (dot(gout_ref[...], logit_grad) * slope).astype(jnp.bfloat16)
            pair = weighted + dot(gin_ref[...], hidden_grad)
            for n, u in enumerate(picked):
                for b in range(K):
                    pair_s[u * K : (u + 1) * K, b * BLK : (b + 1) * BLK] = pair[
                        b * K : (b + 1) * K, n * BLK : (n + 1) * BLK
                    ]
        pair_all = pair_s[...].astype(jnp.bfloat16)
        uacc[column] += dot(pair_all, vec_cat, NT)
        grad = dot(users_t_ref[column], pair_all).astype(jnp.bfloat16)
        grad_t = jnp.concatenate([grad[:, b * BLK : (b + 1) * BLK] for b in range(K)], axis=0)
        acc[...] += dot(grad_t, feat)

    @pl.when(step == pl.num_programs(0) - 1)
    def _():
        width = acc.shape[1] // owners
        height = acc.shape[0] // groups
        share = rows // groups
        out_ref[...] = jnp.zeros_like(out_ref)
        for g in range(groups):
            for s in range(owners):
                out_ref[g, s, 0:height, 0:width] = acc[
                    g * height : (g + 1) * height, s * width : (s + 1) * width
                ].astype(jnp.bfloat16)
                out_ref[g, s, height : height + share, 0:H] = (
                    uacc[s, g * share : (g + 1) * share] * (1.0 / math.sqrt(H))
                ).astype(jnp.bfloat16)


def sum_kernel(
    groups,
    owners,
    in_ref,
    tower_out,
    user_out,
    recv1,
    stage,
    recv2,
    part,
    final,
    send1,
    rsem1,
    send2,
    rsem2,
    send3,
    rsem3,
):
    g = lax.axis_index("blk")
    s = lax.axis_index("shard")
    height = part.shape[0]
    width = tower_out.shape[0]

    barrier = pltpu.get_barrier_semaphore()
    for d in range(1, groups):
        pl.semaphore_signal(
            barrier, inc=1, device_id=(lax.rem(g + d, groups), s),
            device_id_type=pl.DeviceIdType.MESH,
        )
    for d in range(1, owners):
        pl.semaphore_signal(
            barrier, inc=1, device_id=(g, lax.rem(s + d, owners)),
            device_id_type=pl.DeviceIdType.MESH,
        )
    pl.semaphore_wait(barrier, groups + owners - 2)

    copies = []
    for d in range(1, groups):
        to = lax.rem(g + d, groups)
        copy = pltpu.make_async_remote_copy(
            src_ref=in_ref.at[to], dst_ref=recv1.at[d - 1],
            send_sem=send1.at[d - 1], recv_sem=rsem1.at[d - 1],
            device_id=(to, s), device_id_type=pl.DeviceIdType.MESH,
        )
        copy.start()
        copies.append(copy)
    for copy in copies:
        copy.wait()
    total = in_ref[g].astype(jnp.float32)
    for d in range(1, groups):
        total = total + recv1[d - 1].astype(jnp.float32)
    stage[...] = total.astype(jnp.bfloat16)

    copies = []
    for d in range(1, owners):
        to = lax.rem(s + d, owners)
        copy = pltpu.make_async_remote_copy(
            src_ref=stage.at[to], dst_ref=recv2.at[d - 1],
            send_sem=send2.at[d - 1], recv_sem=rsem2.at[d - 1],
            device_id=(g, to), device_id_type=pl.DeviceIdType.MESH,
        )
        copy.start()
        copies.append(copy)
    for copy in copies:
        copy.wait()
    mine = stage[s].astype(jnp.float32)
    for d in range(1, owners):
        mine = mine + recv2[d - 1].astype(jnp.float32)
    user_out[...] = mine[height:, :]
    part[...] = mine[:height, :]

    copies = []
    for d in range(1, groups):
        to = lax.rem(g + d, groups)
        copy = pltpu.make_async_remote_copy(
            src_ref=part, dst_ref=final.at[g],
            send_sem=send3.at[d - 1], recv_sem=rsem3.at[d - 1],
            device_id=(to, s), device_id_type=pl.DeviceIdType.MESH,
        )
        copy.start()
        copies.append(copy)
    final[g] = part[...]
    for copy in copies:
        copy.wait()
    for r in range(groups):
        tower_out[:, r * height : (r + 1) * height] = final[r].T[:width]


def swap(weights):
    return weights.reshape((K, K) + weights.shape[1:]).swapaxes(0, 1).reshape(weights.shape)


def shards(
    item_features,
    tower_weight,
    gate_in,
    gate_in_bias,
    gate_out,
    gate_out_bias,
    user_table,
    user_ids,
    positive_item,
    listed_owner,
    listed_slot,
):
    groups = lax.axis_size("blk")
    owners = lax.axis_size("shard")
    g = lax.axis_index("blk")
    s = lax.axis_index("shard")
    trainers = groups * owners
    listings = listed_slot.shape[0]
    users, picks = positive_item.shape
    table = user_table.shape[0]
    features = item_features.shape[1]
    embed = tower_weight.shape[1]
    hidden = gate_in.shape[1]
    column_users = groups * users
    rows = column_users * K
    circle_part = listings * BLK

    row_match = user_ids[:, None] == jnp.arange(table, dtype=jnp.int32)[None, :]
    user_rows = jnp.dot(
        row_match.astype(jnp.bfloat16), user_table, preferred_element_type=jnp.float32
    ).astype(jnp.bfloat16)
    flat_pos = positive_item.reshape(-1)
    numbers = jnp.concatenate([flat_pos // 128, flat_pos % 128, listed_owner[:, 0], listed_slot])
    number_row = jnp.zeros((1, embed), jnp.bfloat16).at[0, : numbers.shape[0]].set(
        numbers.astype(jnp.bfloat16)
    )
    packet = jnp.concatenate([user_rows, number_row], axis=0)
    packet = jnp.pad(packet, ((0, 16 - users - 1), (0, 0)))
    gathered = lax.all_gather(packet, ("blk", "shard"), axis=0, tiled=False)
    all_users = gathered[:, :users].reshape(groups, owners, users * K, H)
    all_users = all_users.swapaxes(0, 1).reshape(owners, rows, H)
    all_users = (all_users.astype(jnp.float32) * (1.0 / math.sqrt(H))).astype(jnp.bfloat16)
    all_users_t = all_users.swapaxes(1, 2)
    back = gathered[:, users].astype(jnp.float32).astype(jnp.int32)
    span = users * picks
    all_pos = (back[:, :span] * 128 + back[:, span : 2 * span]).reshape(
        groups, owners, users, picks
    )
    all_pos = all_pos.swapaxes(0, 1).reshape(owners, column_users, picks)
    all_owner = back[:, 2 * span : 2 * span + listings].reshape(-1)
    all_slot = back[:, 2 * span + listings : 2 * span + 2 * listings].reshape(-1)

    entries = trainers * listings
    most = -(-trainers * min(CAP, listings) // groups)
    entry = jnp.arange(entries, dtype=jnp.int32)
    own = all_owner == s
    rank = jnp.sum(
        jnp.where(jnp.logical_and(own[None, :], entry[None, :] < entry[:, None]), 1, 0), axis=1
    )
    count = (jnp.sum(own.astype(jnp.int32)) - g + groups - 1) // groups
    place = jnp.minimum(jnp.arange(most, dtype=jnp.int32), jnp.maximum(count - 1, 0))
    chosen = jnp.logical_and(own[None, :], rank[None, :] == place[:, None] * groups + g)

    def choose(values):
        return jnp.sum(jnp.where(chosen, values[None, :], 0), axis=1)

    trainer = entry // listings
    unit_block = choose(all_slot)
    unit_column = choose(trainer % owners)
    unit_base = choose((trainer // owners) * circle_part + (entry % listings) * BLK)

    gin = swap(gate_in)
    gout_t = swap(gate_out.T)
    height = embed // groups
    width = features // owners
    out_rows = height + users * K

    def whole(shape):
        return pl.BlockSpec(shape, lambda i, *_: (0,) * len(shape))

    terms = pl.pallas_call(
        functools.partial(pair_kernel, groups, owners, users),
        grid_spec=pltpu.PrefetchScalarGridSpec(
            num_scalar_prefetch=4,
            grid=(most,),
            in_specs=[
                pl.BlockSpec((BLK, features), lambda i, c, b, *_: (b[i], 0)),
                whole((embed, features)),
                whole((owners, rows, H)),
                whole((owners, H, rows)),
                whole((owners, column_users, picks)),
                whole((K * K, hidden)),
                whole((hidden, K * K)),
                whole((hidden, 1)),
                whole((hidden, K * K)),
                whole((K * K, hidden)),
                whole((K * K, 1)),
            ],
            out_specs=whole((groups, owners, out_rows, LANES)),
            scratch_shapes=[
                pltpu.VMEM((embed, features), jnp.float32),
                pltpu.VMEM((owners, rows, H), jnp.float32),
                pltpu.VMEM((rows, K * BLK), jnp.float32),
                pltpu.VMEM((rows, K * BLK), jnp.float32),
            ],
        ),
        out_shape=jax.ShapeDtypeStruct((groups, owners, out_rows, LANES), jnp.bfloat16),
        compiler_params=pltpu.CompilerParams(
            dimension_semantics=("arbitrary",), vmem_limit_bytes=56 << 20
        ),
    )(
        count.reshape(1),
        unit_block,
        unit_column,
        unit_base,
        item_features,
        tower_weight.T,
        all_users,
        all_users_t,
        all_pos,
        gin,
        gin.T,
        gate_in_bias.astype(jnp.float32)[:, None],
        gout_t.T,
        gout_t,
        swap(gate_out_bias.astype(jnp.float32))[:, None],
    )

    tower_gradient, user_terms = pl.pallas_call(
        functools.partial(sum_kernel, groups, owners),
        out_shape=(
            jax.ShapeDtypeStruct((width, embed), jnp.float32),
            jax.ShapeDtypeStruct((users * K, LANES), jnp.float32),
        ),
        in_specs=[pl.BlockSpec(memory_space=pltpu.VMEM)],
        out_specs=(
            pl.BlockSpec(memory_space=pltpu.VMEM),
            pl.BlockSpec(memory_space=pltpu.VMEM),
        ),
        scratch_shapes=[
            pltpu.VMEM((groups - 1, owners, out_rows, LANES), jnp.bfloat16),
            pltpu.VMEM((owners, out_rows, LANES), jnp.bfloat16),
            pltpu.VMEM((owners - 1, out_rows, LANES), jnp.bfloat16),
            pltpu.VMEM((height, LANES), jnp.float32),
            pltpu.VMEM((groups, height, LANES), jnp.float32),
            pltpu.SemaphoreType.DMA((groups - 1,)),
            pltpu.SemaphoreType.DMA((groups - 1,)),
            pltpu.SemaphoreType.DMA((owners - 1,)),
            pltpu.SemaphoreType.DMA((owners - 1,)),
            pltpu.SemaphoreType.DMA((groups - 1,)),
            pltpu.SemaphoreType.DMA((groups - 1,)),
        ],
        compiler_params=pltpu.CompilerParams(collective_id=0, has_side_effects=True),
    )(terms)

    user_delta = user_terms[:, :H].reshape(users, embed)
    user_gradient = jnp.sum(
        jnp.where(row_match[:, :, None], user_delta[:, None, :], 0.0), axis=0
    )
    return (tower_gradient, user_gradient)


def solution(mesh):
    return jax.shard_map(
        shards,
        mesh=mesh,
        in_specs=(
            P("shard", None),
            P(),
            P(),
            P(),
            P(),
            P(),
            P(("blk", "shard"), None),
            P(("blk", "shard")),
            P(("blk", "shard"), None),
            P(("blk", "shard"), None),
            P(("blk", "shard")),
        ),
        out_specs=(P("shard", None), P(("blk", "shard"), None)),
        check_vma=False,
    )
```

time: 319 us -> 162 us (0.51)
  the two profiles are of different devices: /device:TPU:0 before, /device:TPU:31 now
where the time goes in v1:
time: 162 us; the launch traced here: 160 us
  Pallas kernels  72.9 us (45%)
  blocking collectives  65.7 us (41%)
  local copies, waits for them, and re-layouts  12.6 us (8%)
  other arithmetic  6.06 us (4%)
    all_gather x1, blocking collectives, shards(): gathered = lax.all_gather(packet, ('blk', 'shard'), axis=0, tiled=False)  65.7 us
    pallas_call x1, Pallas kernels, shards(): pl.pallas_call(functools.partial(sum_kernel, groups, owners), out_shape=(...  57.2 us
    pallas_call x1, Pallas kernels, shards(): pl.pallas_call(functools.partial(pair_kernel, groups, owners, users), gri...  15.8 us
    unnamed x13, local copies, waits for them, and re-layouts  3.99 us

profile of v1, /device:TPU:31, one launch (start us, length us, event | category | flops | bytes accessed | tf_op | source)
XLA Modules:
  0.0 159.6 jit_solution(15559341038874080518)
XLA Ops:
  0.6 0.8 reshape.208
  1.5 0.6 compare_reduce_fusion
  2.1 0.7 convert_bitcast_fusion
  2.8 0.7 convert_bitcast_fusion.1
  3.4 0.7 broadcast_select_fusion
  4.1 0.8 convolution_convert_fusion
  5.0 65.7 %all-gather = bf16[512,512]{1,0:T(8,128)(2,1)S(1)} all-gather(bf16[16,512]{1,0:T(8,128)(2,1)S(1)} %pad.9), channel_id=2, replica_groups=mesh['blk'=4,'shard'=8] {'blk','shard'}, dimensions={0}, use_global_device_ids=true | all-gather | bytes 540672 | tf_op jit(solution)/shard_map/all_gather | solution.py:265
  70.7 0.1 fusion
  70.9 0.6 convert_reduce_fusion
  72.2 0.1 eq.54
  72.3 0.1 select_reduce_fusion.1
  72.4 0.1 broadcast_in_dim.75
  72.5 0.8 select_reduce_fusion.2
  73.4 0.2 mul.52
  73.6 0.8 copy.47
  74.4 0.1 slice_add_fusion
  74.5 0.1 reshape.210
  74.6 0.6 copy.48
  75.2 0.7 copy.62
  75.9 0.7 copy.50
  76.7 0.7 copy.63
  77.4 0.7 copy.54.gout_ref
  78.1 2.3 %copy.45 = bf16[1024,512]{0,1:T(8,128)(2,1)} copy(bf16[1024,512]{1,0:T(8,128)(2,1)} %param.14) | data formatting | bytes 2097152 | tf_op args[1]
  80.4 0.7 bitcast_convert_fusion
  81.0 0.7 copy.53.gin_b_ref
  81.8 0.7 reshape.219
  82.6 0.7 reshape.221.gout_b_ref
  83.3 15.8 %shard_map.122.in_ref = bf16[4,8,160,128]{3,2,1,0:T(8,128)(2,1)} custom-call(s32[1]{0:T(128)} %bitcast.5.count_ref, s32[16]{0:T(128)} %get-tuple-element.20.block_ref, s32[16]{0:T(128)} %get-tuple-element.19.column_ref, s32[16]{0:T(128)} %get-tuple-element.18.base_ref, bf16[4096,1024]{1,0:T(8,128)(2,1)} %feat_ref.1, bf16[512,1024]{1,0:T(8,128)(2,1)} %bitcast.44, ...), custom_call_target="tpu_custom_call" | custom-call | tf_op jit(solution)/shard_map/pallas_call | solution.py:307
  99.0 57.2 %shard_map.123 = (f32[128,512]{1,0:T(8,128)}, f32[32,128]{1,0:T(8,128)}) custom-call(bf16[4,8,160,128]{3,2,1,0:T(8,128)(2,1)} %shard_map.122.in_ref), custom_call_target="tpu_custom_call" | custom-call | tf_op jit(solution)/shard_map/pallas_call | solution.py:355
  156.2 0.8 broadcast_in_dim.83
  157.1 0.8 select_reduce_fusion
  157.9 1.7 %copy.65 = f32[128,512]{1,0:T(8,128)} copy(f32[128,512]{1,0:T(8,128)} %get-tuple-element.32) | data formatting | bytes 524288
  (20 shorter events, 0.3 us)
Async XLA Ops:
  0.6 3.5 %copy-start = (bf16[128,512]{1,0:T(8,128)(2,1)S(1)}, bf16[128,512]{1,0:T(8,128)(2,1)}, u32[]{:S(2)}) copy-start(bf16[128,512]{1,0:T(8,128)(2,1)} %param.19) | copy-start | bytes 393220
  73.4 83.6 %copy-start.4 = (s32[4]{0:T(128)S(1)}, s32[4]{0:T(128)}, u32[]{:S(2)}) copy-start(s32[4]{0:T(128)} %param.20) | copy-start | bytes 52
  73.6 9.6 %copy-start.1 = (bf16[8,4,32,64]{3,2,1,0:T(8,128)(2,1)}, bf16[8,4,32,64]{3,2,1,0:T(8,128)(2,1)S(1)}, u32[]{:S(2)}) copy-start(bf16[8,4,32,64]{3,2,1,0:T(8,128)(2,1)S(1)} %copy.46) | copy-start | bytes 393220
  75.9 7.3 %copy-start.2 = (bf16[8,8,128]{2,1,0:T(8,128)(2,1)}, bf16[8,8,128]{2,1,0:T(8,128)(2,1)S(1)}, u32[]{:S(2)}) copy-start(bf16[8,8,128]{2,1,0:T(8,128)(2,1)S(1)} %copy.62) | copy-start | bytes 49156
  77.4 5.9 %copy-start.3 = (bf16[8,8,128]{2,0,1:T(8,128)(2,1)}, bf16[8,8,128]{2,0,1:T(8,128)(2,1)S(1)}, u32[]{:S(2)}) copy-start(bf16[8,8,128]{2,0,1:T(8,128)(2,1)S(1)} %copy.63) | copy-start | bytes 49156

commit v2 on v1

--- a/solution.py
+++ b/solution.py
@@ -37,20 +37,24 @@
     base_ref,
     feat_ref,
     tower_ref,
-    users_ref,
-    users_t_ref,
-    pos_ref,
+    packet_ref,
+    gin_in,
+    gin_b_in,
+    gout_in,
+    gout_b_in,
+    out_ref,
+    acc,
+    uacc,
+    logit_s,
+    pair_s,
     gin_ref,
     gin_t_ref,
     gin_b_ref,
     gout_ref,
     gout_t_ref,
     gout_b_ref,
-    out_ref,
-    acc,
-    uacc,
-    logit_s,
-    pair_s,
+    *,
+    picks,
 ):
     step = pl.program_id(0)
     column_users = groups * users
@@ -60,6 +64,22 @@
     def _():
         acc[...] = jnp.zeros_like(acc)
         uacc[...] = jnp.zeros_like(uacc)
+        pairs = K * K
+        to = lax.broadcasted_iota(jnp.int32, (pairs, pairs), 0)
+        of = lax.broadcasted_iota(jnp.int32, (pairs, pairs), 1)
+        turn = jnp.where(of == (to % K) * K + to // K, 1.0, 0.0).astype(jnp.bfloat16)
+        gin = dot(turn, gin_in[...])
+        gin_ref[...] = gin.astype(jnp.bfloat16)
+        gin_t_ref[...] = gin.T.astype(jnp.bfloat16)
+        gout = dot(gout_in[...], turn, NT)
+        gout_ref[...] = gout.astype(jnp.bfloat16)
+        gout_t_ref[...] = gout.T.astype(jnp.bfloat16)
+
+        def stand(row):
+            return jnp.broadcast_to(row.astype(jnp.float32), (LANES, row.shape[1])).T
+
+        gin_b_ref[...] = stand(gin_b_in[...])[:, 0:1]
+        gout_b_ref[...] = dot(turn, stand(gout_b_in[...]).astype(jnp.bfloat16))[:, 0:1]
 
     @pl.when(step < count_ref[0])
     def _():
@@ -68,8 +88,15 @@
         feat = feat_ref[...]
         vec_t = dot(tower_ref[...], feat, NT).astype(jnp.bfloat16)
         vec_cat = jnp.concatenate([vec_t[b * H : (b + 1) * H] for b in range(K)], axis=1)
-        logit_s[...] = dot(users_ref[column], vec_cat)
-        pos = pos_ref[column]
+        packets = [packet_ref[g, column] for g in range(groups)]
+        packed = jnp.concatenate(packets, axis=0)
+        vectors = packed[:, :H]
+        vectors_t = packed.astype(jnp.float32).T[:H].astype(jnp.bfloat16)
+        logit_s[...] = dot(vectors, vec_cat)
+        numbers = jnp.concatenate(
+            [part.astype(jnp.float32)[:users, H : H + 2 * picks] for part in packets], axis=0
+        )
+        pos = (numbers[:, :picks] * 128.0 + numbers[:, picks:]).astype(jnp.int32)
         place = base + lax.broadcasted_iota(jnp.int32, (column_users, BLK), 1)
         hit = pos[:, 0:1] == place
         for k in range(1, pos.shape[1]):
@@ -111,7 +138,7 @@
                     ]
         pair_all = pair_s[...].astype(jnp.bfloat16)
         uacc[column] += dot(pair_all, vec_cat, NT)
-        grad = dot(users_t_ref[column], pair_all).astype(jnp.bfloat16)
+        grad = dot(vectors_t, pair_all).astype(jnp.bfloat16)
         grad_t = jnp.concatenate([grad[:, b * BLK : (b + 1) * BLK] for b in range(K)], axis=0)
         acc[...] += dot(grad_t, feat)
 
@@ -219,8 +246,49 @@
         tower_out[:, r * height : (r + 1) * height] = final[r].T[:width]
 
 
-def swap(weights):
-    return weights.reshape((K, K) + weights.shape[1:]).swapaxes(0, 1).reshape(weights.shape)
+def gather_kernel(groups, owners, in_ref, out_ref, held, own_sem, send1, rsem1, send2, rsem2):
+    g = lax.axis_index("blk")
+    s = lax.axis_index("shard")
+    barrier = pltpu.get_barrier_semaphore()
+    for d in range(1, groups):
+        pl.semaphore_signal(
+            barrier, inc=1, device_id=(lax.rem(g + d, groups), s),
+            device_id_type=pl.DeviceIdType.MESH,
+        )
+    for d in range(1, owners):
+        pl.semaphore_signal(
+            barrier, inc=1, device_id=(g, lax.rem(s + d, owners)),
+            device_id_type=pl.DeviceIdType.MESH,
+        )
+    pl.semaphore_wait(barrier, groups + owners - 2)
+
+    copies = []
+    for d in range(1, owners):
+        copy = pltpu.make_async_remote_copy(
+            src_ref=in_ref, dst_ref=held.at[g, s],
+            send_sem=send1.at[d - 1], recv_sem=rsem1.at[d - 1],
+            device_id=(g, lax.rem(s + d, owners)), device_id_type=pl.DeviceIdType.MESH,
+        )
+        copy.start()
+        copies.append(copy)
+    own = pltpu.make_async_copy(in_ref, held.at[g, s], own_sem)
+    own.start()
+    own.wait()
+    for copy in copies:
+        copy.wait()
+
+    copies = []
+    for d in range(1, groups):
+        copy = pltpu.make_async_remote_copy(
+            src_ref=held.at[g], dst_ref=held.at[g],
+            send_sem=send2.at[d - 1], recv_sem=rsem2.at[d - 1],
+            device_id=(lax.rem(g + d, groups), s), device_id_type=pl.DeviceIdType.MESH,
+        )
+        copy.start()
+        copies.append(copy)
+    for copy in copies:
+        copy.wait()
+    out_ref[...] = held[...]
 
 
 def shards(
@@ -255,26 +323,33 @@
     user_rows = jnp.dot(
         row_match.astype(jnp.bfloat16), user_table, preferred_element_type=jnp.float32
     ).astype(jnp.bfloat16)
-    flat_pos = positive_item.reshape(-1)
-    numbers = jnp.concatenate([flat_pos // 128, flat_pos % 128, listed_owner[:, 0], listed_slot])
-    number_row = jnp.zeros((1, embed), jnp.bfloat16).at[0, : numbers.shape[0]].set(
-        numbers.astype(jnp.bfloat16)
-    )
-    packet = jnp.concatenate([user_rows, number_row], axis=0)
-    packet = jnp.pad(packet, ((0, 16 - users - 1), (0, 0)))
-    gathered = lax.all_gather(packet, ("blk", "shard"), axis=0, tiled=False)
-    all_users = gathered[:, :users].reshape(groups, owners, users * K, H)
-    all_users = all_users.swapaxes(0, 1).reshape(owners, rows, H)
-    all_users = (all_users.astype(jnp.float32) * (1.0 / math.sqrt(H))).astype(jnp.bfloat16)
-    all_users_t = all_users.swapaxes(1, 2)
-    back = gathered[:, users].astype(jnp.float32).astype(jnp.int32)
-    span = users * picks
-    all_pos = (back[:, :span] * 128 + back[:, span : 2 * span]).reshape(
-        groups, owners, users, picks
-    )
-    all_pos = all_pos.swapaxes(0, 1).reshape(owners, column_users, picks)
-    all_owner = back[:, 2 * span : 2 * span + listings].reshape(-1)
-    all_slot = back[:, 2 * span + listings : 2 * span + 2 * listings].reshape(-1)
+    vectors = (user_rows.astype(jnp.float32) * (1.0 / math.sqrt(H))).astype(jnp.bfloat16)
+    vectors = vectors.reshape(users * K, H)
+    digits = jnp.concatenate([positive_item // 128, positive_item % 128], axis=1)
+    lines = jnp.zeros((users * K, H), jnp.int32)
+    lines = lax.dynamic_update_slice(lines, digits, (0, 0))
+    lines = lax.dynamic_update_slice(lines, listed_owner.T, (users, 0))
+    lines = lax.dynamic_update_slice(lines, listed_slot[None, :], (users + 1, 0))
+    packet = jnp.concatenate([vectors, lines.astype(jnp.bfloat16)], axis=1)
+    gathered = pl.pallas_call(
+        functools.partial(gather_kernel, groups, owners),
+        out_shape=jax.ShapeDtypeStruct((groups, owners, users * K, 2 * H), jnp.bfloat16),
+        in_specs=[pl.BlockSpec(memory_space=pltpu.VMEM)],
+        out_specs=pl.BlockSpec(memory_space=pltpu.VMEM),
+        scratch_shapes=[
+            pltpu.VMEM((groups, owners, users * K, 2 * H), jnp.bfloat16),
+            pltpu.SemaphoreType.DMA,
+            pltpu.SemaphoreType.DMA((owners - 1,)),
+            pltpu.SemaphoreType.DMA((owners - 1,)),
+            pltpu.SemaphoreType.DMA((groups - 1,)),
+            pltpu.SemaphoreType.DMA((groups - 1,)),
+        ],
+        compiler_params=pltpu.CompilerParams(collective_id=1, has_side_effects=True),
+    )(packet)
+    asked = gathered[:, :, users : users + 2, H : H + listings].astype(jnp.float32)
+    asked = asked.astype(jnp.int32)
+    all_owner = asked[:, :, 0].reshape(-1)
+    all_slot = asked[:, :, 1].reshape(-1)
 
     entries = trainers * listings
     most = -(-trainers * min(CAP, listings) // groups)
@@ -295,8 +370,6 @@
     unit_column = choose(trainer % owners)
     unit_base = choose((trainer // owners) * circle_part + (entry % listings) * BLK)
 
-    gin = swap(gate_in)
-    gout_t = swap(gate_out.T)
     height = embed // groups
     width = features // owners
     out_rows = height + users * K
@@ -305,22 +378,18 @@
         return pl.BlockSpec(shape, lambda i, *_: (0,) * len(shape))
 
     terms = pl.pallas_call(
-        functools.partial(pair_kernel, groups, owners, users),
+        functools.partial(pair_kernel, groups, owners, users, picks=picks),
         grid_spec=pltpu.PrefetchScalarGridSpec(
             num_scalar_prefetch=4,
             grid=(most,),
             in_specs=[
                 pl.BlockSpec((BLK, features), lambda i, c, b, *_: (b[i], 0)),
                 whole((embed, features)),
-                whole((owners, rows, H)),
-                whole((owners, H, rows)),
-                whole((owners, column_users, picks)),
+                whole((groups, owners, users * K, 2 * H)),
                 whole((K * K, hidden)),
+                whole((1, hidden)),
                 whole((hidden, K * K)),
-                whole((hidden, 1)),
-                whole((hidden, K * K)),
-                whole((K * K, hidden)),
-                whole((K * K, 1)),
+                whole((1, K * K)),
             ],
             out_specs=whole((groups, owners, out_rows, LANES)),
             scratch_shapes=[
@@ -328,6 +397,12 @@
                 pltpu.VMEM((owners, rows, H), jnp.float32),
                 pltpu.VMEM((rows, K * BLK), jnp.float32),
                 pltpu.VMEM((rows, K * BLK), jnp.float32),
+                pltpu.VMEM((K * K, hidden), jnp.bfloat16),
+                pltpu.VMEM((hidden, K * K), jnp.bfloat16),
+                pltpu.VMEM((hidden, 1), jnp.float32),
+                pltpu.VMEM((hidden, K * K), jnp.bfloat16),
+                pltpu.VMEM((K * K, hidden), jnp.bfloat16),
+                pltpu.VMEM((K * K, 1), jnp.float32),
             ],
         ),
         out_shape=jax.ShapeDtypeStruct((groups, owners, out_rows, LANES), jnp.bfloat16),
@@ -341,15 +416,11 @@
         unit_base,
         item_features,
         tower_weight.T,
-        all_users,
-        all_users_t,
-        all_pos,
-        gin,
-        gin.T,
-        gate_in_bias.astype(jnp.float32)[:, None],
-        gout_t.T,
-        gout_t,
-        swap(gate_out_bias.astype(jnp.float32))[:, None],
+        gathered,
+        gate_in,
+        gate_in_bias[None, :],
+        gate_out,
+        gate_out_bias[None, :],
     )
 
     tower_gradient, user_terms = pl.pallas_call(

time: 162 us -> 103 us (0.64)
  the two profiles are of different devices: /device:TPU:31 before, /device:TPU:0 now
where the time goes in v2:
time: 103 us; the launch traced here: 101 us
  Pallas kernels  85.7 us (83%)
  local copies, waits for them, and re-layouts  8.03 us (8%)
  other arithmetic  5 us (5%)
  between operations  1.39 us (1%)
    pallas_call x1, Pallas kernels, shards(): pl.pallas_call(functools.partial(pair_kernel, groups, owners, users, pick...  41.8 us
    pallas_call x1, Pallas kernels, shards(): pl.pallas_call(functools.partial(sum_kernel, groups, owners), out_shape=(...  30 us
    pallas_call x1, Pallas kernels, shards(): pl.pallas_call(functools.partial(gather_kernel, groups, owners), out_shap...  13.9 us
    unnamed x7, local copies, waits for them, and re-layouts  5.4 us

profile of v2, /device:TPU:0, one launch (start us, length us, event | category | flops | bytes accessed | tf_op | source)
XLA Modules:
  0.0 101.0 jit_solution(10423945520243217402)
XLA Ops:
  0.6 0.0 copy-start
  0.6 0.0 copy-start.1
  0.7 0.7 add_select_fusion.1
  1.4 0.1 pad_add_fusion
  1.5 0.7 dynamic_update_slice.10
  2.2 0.8 dynamic_update_slice.11
  3.0 0.0 copy-done
  3.0 0.8 fusion.2
  3.9 0.1 reshape.100
  4.0 0.7 pad_maximum_fusion.in_ref
  4.6 13.9 %shard_map.122.packet_ref = bf16[4,8,32,128]{3,2,1,0:T(8,128)(2,1)} custom-call(bf16[32,128]{1,0:T(8,128)(2,1)} %pad_maximum_fusion.in_ref), custom_call_target="tpu_custom_call" | custom-call | tf_op jit(solution)/shard_map/pallas_call | solution.py:334
  18.6 0.9 convert_convert_fusion
  19.5 0.7 slice_reduce_fusion
  20.9 0.1 broadcast_in_dim.80
  21.0 0.1 compare_reduce_fusion
  21.1 0.1 eq.54
  21.2 0.1 select_reduce_fusion.1
  21.3 0.8 select_reduce_fusion.2
  22.1 2.3 %copy.17 = bf16[1024,512]{0,1:T(8,128)(2,1)} copy(bf16[1024,512]{1,0:T(8,128)(2,1)} %param.12) | data formatting | bytes 2097152 | tf_op args[1]
  24.4 1.4 %copy.18.gout_in = bf16[128,64]{1,0:T(8,128)(2,1)} copy(bf16[128,64]{0,1:T(8,128)(2,1)} %param.15) | data formatting | bytes 32768 | tf_op args[4]
  25.8 41.8 %shard_map.123.in_ref = bf16[4,8,160,128]{3,2,1,0:T(8,128)(2,1)} custom-call(s32[1]{0:T(128)} %bitcast.2.count_ref, s32[16]{0:T(128)} %get-tuple-element.10.block_ref, s32[16]{0:T(128)} %get-tuple-element.9.column_ref, s32[16]{0:T(128)} %get-tuple-element.8.base_ref, bf16[4096,1024]{1,0:T(8,128)(2,1)} %feat_ref.1, bf16[512,1024]{1,0:T(8,128)(2,1)} %bitcast.8, ...), custom_call_target="tpu_custom_call" | custom-call | tf_op jit(solution)/shard_map/pallas_call | solution.py:380
  67.6 30.0 %shard_map.124 = (f32[128,512]{1,0:T(8,128)}, f32[32,128]{1,0:T(8,128)}) custom-call(bf16[4,8,160,128]{3,2,1,0:T(8,128)(2,1)} %shard_map.123.in_ref), custom_call_target="tpu_custom_call" | custom-call | tf_op jit(solution)/shard_map/pallas_call | solution.py:426
  97.6 0.8 broadcast_in_dim.88
  98.4 0.0 copy-done.1
  98.4 0.1 iota_compare_fusion.1
  98.5 0.8 select_reduce_fusion
  99.3 1.7 %copy.22 = f32[128,512]{1,0:T(8,128)} copy(f32[128,512]{1,0:T(8,128)} %get-tuple-element.17) | data formatting | bytes 524288
  (4 shorter events, 0.0 us)
Async XLA Ops:
  0.6 2.4 %copy-start = (bf16[128,512]{1,0:T(8,128)(2,1)S(1)}, bf16[128,512]{1,0:T(8,128)(2,1)}, u32[]{:S(2)}) copy-start(bf16[128,512]{1,0:T(8,128)(2,1)} %param.17) | copy-start | bytes 393220
  0.6 97.7 %copy-start.1 = (s32[4]{0:T(128)S(1)}, s32[4]{0:T(128)}, u32[]{:S(2)}) copy-start(s32[4]{0:T(128)} %param.18) | copy-start | bytes 52

commit v3 on v2

--- a/solution.py
+++ b/solution.py
@@ -13,7 +13,8 @@
 BLK = 128
 CAP = 2
 LANES = 128
-CHUNK = 4
+CHUNK = 16
+CORES = 2
 
 NN = (((1,), (0,)), ((), ()))
 NT = (((1,), (1,)), ((), ()))
@@ -71,9 +72,9 @@
         gin = dot(turn, gin_in[...])
         gin_ref[...] = gin.astype(jnp.bfloat16)
         gin_t_ref[...] = gin.T.astype(jnp.bfloat16)
-        gout = dot(gout_in[...], turn, NT)
-        gout_ref[...] = gout.astype(jnp.bfloat16)
-        gout_t_ref[...] = gout.T.astype(jnp.bfloat16)
+        gout_t = dot(turn, gout_in[...])
+        gout_t_ref[...] = gout_t.astype(jnp.bfloat16)
+        gout_ref[...] = gout_t.T.astype(jnp.bfloat16)
 
         def stand(row):
             return jnp.broadcast_to(row.astype(jnp.float32), (LANES, row.shape[1])).T
@@ -164,11 +165,15 @@
     in_ref,
     tower_out,
     user_out,
+    recv0,
+    both,
     recv1,
     stage,
     recv2,
     part,
     final,
+    send0,
+    rsem0,
     send1,
     rsem1,
     send2,
@@ -194,20 +199,39 @@
         )
     pl.semaphore_wait(barrier, groups + owners - 2)
 
+    half = groups // CORES
+    core = lax.rem(g, CORES)
+    chip = g // CORES
+    other = chip * CORES + (CORES - 1) - core
+    first = []
+    for d in range(1, half + 1):
+        at = lax.rem(chip + d, half)
+        copy = pltpu.make_async_remote_copy(
+            src_ref=in_ref.at[at * CORES + (CORES - 1) - core], dst_ref=recv0.at[d - 1],
+            send_sem=send0.at[d - 1], recv_sem=rsem0.at[d - 1],
+            device_id=(other, s), device_id_type=pl.DeviceIdType.MESH,
+        )
+        copy.start()
+        first.append(copy)
     copies = []
-    for d in range(1, groups):
-        to = lax.rem(g + d, groups)
+    for d in range(1, half):
+        to = lax.rem(chip + d, half) * CORES + core
+        first[d - 1].wait()
+        both[d - 1] = (
+            in_ref[to].astype(jnp.float32) + recv0[d - 1].astype(jnp.float32)
+        ).astype(jnp.bfloat16)
         copy = pltpu.make_async_remote_copy(
-            src_ref=in_ref.at[to], dst_ref=recv1.at[d - 1],
+            src_ref=both.at[d - 1], dst_ref=recv1.at[d - 1],
             send_sem=send1.at[d - 1], recv_sem=rsem1.at[d - 1],
             device_id=(to, s), device_id_type=pl.DeviceIdType.MESH,
         )
         copy.start()
         copies.append(copy)
+    first[half - 1].wait()
     for copy in copies:
         copy.wait()
-    total = in_ref[g].astype(jnp.float32)
-    for d in range(1, groups):
+    total = in_ref[g].astype(jnp.float32) + recv0[half - 1].astype(jnp.float32)
+    for d in range(1, half):
         total = total + recv1[d - 1].astype(jnp.float32)
     stage[...] = total.astype(jnp.bfloat16)
 
@@ -246,7 +270,9 @@
         tower_out[:, r * height : (r + 1) * height] = final[r].T[:width]
 
 
-def gather_kernel(groups, owners, in_ref, out_ref, held, own_sem, send1, rsem1, send2, rsem2):
+def gather_kernel(
+    groups, owners, in_ref, tower_ref, out_ref, tower_t_ref, held, own_sem, send1, rsem1, send2, rsem2
+):
     g = lax.axis_index("blk")
     s = lax.axis_index("shard")
     barrier = pltpu.get_barrier_semaphore()
@@ -273,6 +299,7 @@
         copies.append(copy)
     own = pltpu.make_async_copy(in_ref, held.at[g, s], own_sem)
     own.start()
+    tower_t_ref[...] = tower_ref[...].T
     own.wait()
     for copy in copies:
         copy.wait()
@@ -331,11 +358,14 @@
     lines = lax.dynamic_update_slice(lines, listed_owner.T, (users, 0))
     lines = lax.dynamic_update_slice(lines, listed_slot[None, :], (users + 1, 0))
     packet = jnp.concatenate([vectors, lines.astype(jnp.bfloat16)], axis=1)
-    gathered = pl.pallas_call(
+    gathered, tower_t = pl.pallas_call(
         functools.partial(gather_kernel, groups, owners),
-        out_shape=jax.ShapeDtypeStruct((groups, owners, users * K, 2 * H), jnp.bfloat16),
-        in_specs=[pl.BlockSpec(memory_space=pltpu.VMEM)],
-        out_specs=pl.BlockSpec(memory_space=pltpu.VMEM),
+        out_shape=(
+            jax.ShapeDtypeStruct((groups, owners, users * K, 2 * H), jnp.bfloat16),
+            jax.ShapeDtypeStruct((embed, features), jnp.bfloat16),
+        ),
+        in_specs=[pl.BlockSpec(memory_space=pltpu.VMEM)] * 2,
+        out_specs=(pl.BlockSpec(memory_space=pltpu.VMEM),) * 2,
         scratch_shapes=[
             pltpu.VMEM((groups, owners, users * K, 2 * H), jnp.bfloat16),
             pltpu.SemaphoreType.DMA,
@@ -345,7 +375,7 @@
             pltpu.SemaphoreType.DMA((groups - 1,)),
         ],
         compiler_params=pltpu.CompilerParams(collective_id=1, has_side_effects=True),
-    )(packet)
+    )(packet, tower_weight)
     asked = gathered[:, :, users : users + 2, H : H + listings].astype(jnp.float32)
     asked = asked.astype(jnp.int32)
     all_owner = asked[:, :, 0].reshape(-1)
@@ -388,7 +418,7 @@
                 whole((groups, owners, users * K, 2 * H)),
                 whole((K * K, hidden)),
                 whole((1, hidden)),
-                whole((hidden, K * K)),
+                whole((K * K, hidden)),
                 whole((1, K * K)),
             ],
             out_specs=whole((groups, owners, out_rows, LANES)),
@@ -415,11 +445,11 @@
         unit_column,
         unit_base,
         item_features,
-        tower_weight.T,
+        tower_t,
         gathered,
         gate_in,
         gate_in_bias[None, :],
-        gate_out,
+        gate_out.T,
         gate_out_bias[None, :],
     )
 
@@ -435,13 +465,17 @@
             pl.BlockSpec(memory_space=pltpu.VMEM),
         ),
         scratch_shapes=[
-            pltpu.VMEM((groups - 1, owners, out_rows, LANES), jnp.bfloat16),
+            pltpu.VMEM((groups // CORES, owners, out_rows, LANES), jnp.bfloat16),
+            pltpu.VMEM((groups // CORES - 1, owners, out_rows, LANES), jnp.bfloat16),
+            pltpu.VMEM((groups // CORES - 1, owners, out_rows, LANES), jnp.bfloat16),
             pltpu.VMEM((owners, out_rows, LANES), jnp.bfloat16),
             pltpu.VMEM((owners - 1, out_rows, LANES), jnp.bfloat16),
             pltpu.VMEM((height, LANES), jnp.float32),
             pltpu.VMEM((groups, height, LANES), jnp.float32),
-            pltpu.SemaphoreType.DMA((groups - 1,)),
-            pltpu.SemaphoreType.DMA((groups - 1,)),
+            pltpu.SemaphoreType.DMA((groups // CORES,)),
+            pltpu.SemaphoreType.DMA((groups // CORES,)),
+            pltpu.SemaphoreType.DMA((groups // CORES - 1,)),
+            pltpu.SemaphoreType.DMA((groups // CORES - 1,)),
             pltpu.SemaphoreType.DMA((owners - 1,)),
             pltpu.SemaphoreType.DMA((owners - 1,)),
             pltpu.SemaphoreType.DMA((groups - 1,)),

time: 103 us -> 80.7 us (0.78); the launches traced: 101 us -> 80.4 us
  Pallas kernels: 85.7 us -> 68.9 us
  local copies, waits for them, and re-layouts: 8.03 us -> 4.32 us
    pallas_call x1, Pallas kernels: 41.8 us -> 27.9 us  [shards(): pl.pallas_call(functools.partial(pair_kernel, groups, owners, users, pick...]
    pallas_call x1, Pallas kernels: 30 us -> 26.2 us  [shards(): pl.pallas_call(functools.partial(sum_kernel, groups, owners), out_shape=(...]
    unnamed x7 -> x5, local copies, waits for them, and re-layouts: 5.4 us -> 1.69 us
where the time goes in v3:
time: 80.7 us; the launch traced here: 80.4 us
  Pallas kernels  68.9 us (85%)
  other arithmetic  5.03 us (6%)
  local copies, waits for them, and re-layouts  4.32 us (5%)
  between operations  1.39 us (2%)
  matrix products  0.84 us (1%)
    pallas_call x1, Pallas kernels, shards(): pl.pallas_call(functools.partial(pair_kernel, groups, owners, users, pick...  27.9 us
    pallas_call x1, Pallas kernels, shards(): pl.pallas_call(functools.partial(sum_kernel, groups, owners), out_shape=(...  26.2 us
    pallas_call x1, Pallas kernels, shards(): pl.pallas_call(functools.partial(gather_kernel, groups, owners), out_shap...  14.8 us
    unnamed x5, local copies, waits for them, and re-layouts  1.69 us

profile of v3, /device:TPU:0, one launch (start us, length us, event | category | flops | bytes accessed | tf_op | source)
XLA Modules:
  0.0 80.4 jit_solution(14785370852617856003)
XLA Ops:
  0.6 0.0 copy-start
  0.6 0.0 copy-start.1
  0.7 0.7 add_select_fusion.1
  1.4 0.1 pad_add_fusion
  1.5 0.7 dynamic_update_slice.10
  2.2 0.8 dynamic_update_slice.11
  3.0 0.0 copy-done
  3.0 0.8 %fusion.2 = bf16[4,512]{1,0:T(4,128)(2,1)S(1)} fusion(bf16[128,512]{1,0:T(8,128)(2,1)S(1)} %copy-done, s32[4]{0:T(128)} %param.18), kind=kOutput, calls=%fused_computation.3 | convolution fusion | flops 532992 | bytes 135184 | tf_op jit(solution)/shard_map/dot_general | solution.py:350
  3.9 0.1 reshape.100
  4.0 0.7 pad_maximum_fusion.in_ref
  4.6 14.8 %shard_map.122 = (bf16[4,8,32,128]{3,2,1,0:T(8,128)(2,1)}, bf16[512,1024]{1,0:T(8,128)(2,1)}) custom-call(bf16[32,128]{1,0:T(8,128)(2,1)} %pad_maximum_fusion.in_ref, bf16[1024,512]{1,0:T(8,128)(2,1)} %tower_ref.1), custom_call_target="tpu_custom_call" | custom-call | tf_op jit(solution)/shard_map/pallas_call | solution.py:361
  19.5 0.9 %convert_convert_fusion = s32[4,8,2,4]{3,2,1,0:T(2,128)S(1)} fusion(bf16[4,8,32,128]{3,2,1,0:T(8,128)(2,1)} %get-tuple-element.6.packet_ref), kind=kLoop, calls=%fused_computation.10 | loop fusion | flops 512 | bytes 1536 | tf_op jit(solution)/shard_map/convert_element_type | solution.py:380
  20.4 0.7 slice_reduce_fusion
  21.8 0.1 broadcast_in_dim.80
  21.9 0.1 compare_reduce_fusion
  22.0 0.1 eq.54
  22.1 0.1 select_reduce_fusion.1
  22.2 0.8 select_reduce_fusion.2
  23.0 27.9 %shard_map.123.in_ref = bf16[4,8,160,128]{3,2,1,0:T(8,128)(2,1)} custom-call(s32[1]{0:T(128)} %bitcast.2.count_ref, s32[16]{0:T(128)} %get-tuple-element.14.block_ref, s32[16]{0:T(128)} %get-tuple-element.13.column_ref, s32[16]{0:T(128)} %get-tuple-element.12.base_ref, bf16[4096,1024]{1,0:T(8,128)(2,1)} %feat_ref.1, ...), custom_call_target="tpu_custom_call" | custom-call | tf_op jit(solution)/shard_map/pallas_call | solution.py:410
  50.9 26.2 %shard_map.124 = (f32[128,512]{1,0:T(8,128)}, f32[32,128]{1,0:T(8,128)}) custom-call(bf16[4,8,160,128]{3,2,1,0:T(8,128)(2,1)} %shard_map.123.in_ref), custom_call_target="tpu_custom_call" | custom-call | tf_op jit(solution)/shard_map/pallas_call | solution.py:456
  77.1 0.8 broadcast_in_dim.88
  77.8 0.0 copy-done.1
  77.9 0.1 iota_compare_fusion.1
  77.9 0.8 %select_reduce_fusion = f32[128,512]{1,0:T(8,128)} fusion(f32[4,512]{1,0:T(4,128)S(1)} %broadcast_in_dim.88, pred[4,128]{1,0:T(4,128)(4,1)S(1)} %iota_compare_fusion.1), kind=kLoop, calls=%fused_computation.4 | loop fusion | flops 458752 | bytes 270848 | tf_op jit(solution)/shard_map/reduce_sum | solution.py:488
  78.8 1.7 %copy.16 = f32[128,512]{1,0:T(8,128)} copy(f32[128,512]{1,0:T(8,128)} %get-tuple-element.21) | data formatting | bytes 524288
  (4 shorter events, 0.0 us)
Async XLA Ops:
  0.6 2.4 %copy-start = (bf16[128,512]{1,0:T(8,128)(2,1)S(1)}, bf16[128,512]{1,0:T(8,128)(2,1)}, u32[]{:S(2)}) copy-start(bf16[128,512]{1,0:T(8,128)(2,1)} %param.17) | copy-start | bytes 393220
  0.6 77.2 %copy-start.1 = (s32[4]{0:T(128)S(1)}, s32[4]{0:T(128)}, u32[]{:S(2)}) copy-start(s32[4]{0:T(128)} %param.18) | copy-start | bytes 52
